TPU v7x, 32 devices: a whole 2x2x4 slice. The times are simulated.
32 devices in a mesh: patch: 8 (over y, x, core), group: 4 (over z).
Axes of the slice: x: 2, y: 2, z: 4, core: 2. Of those that a mesh axis runs over, the one named last changes fastest.
Arguments:
- grid_latent: bfloat16 [16384, 512], P(('patch', 'group')), may hold values from -6 to 6
- mesh_latent: bfloat16 [8192, 512], P(('patch', 'group')), may hold values from -6 to 6
- cotangent: bfloat16 [8192, 512], P(('patch', 'group')), may hold values from -6 to 6
- halo_rows: int32 [8192], P(('patch', 'group')), may hold values from 0 to 511
- encoder_sender: int32 [24576], P(('patch', 'group')), may hold values from 0 to 767
- encoder_target: int32 [24576], P(('patch', 'group')), may hold values from 0 to 255
- encoder_count: int32 [32], P(('patch', 'group')), may hold values from 96 to 768, as said below
- process_sender: int32 [24576], P(('patch', 'group')), may hold values from 0 to 319
- process_target: int32 [24576], P(('patch', 'group')), may hold values from 0 to 255
- process_count: int32 [32], P(('patch', 'group')), may hold values from 96 to 768, as said below
- encoder_source: bfloat16 [512, 512], replicated, may hold values from -0.25 to 0.25
- encoder_dest: bfloat16 [512, 512], replicated, may hold values from -0.25 to 0.25
- encoder_output: bfloat16 [512, 512], replicated, may hold values from -0.25 to 0.25
- encoder_gain: float32 [512], replicated, may hold values from 0.5 to 1.5
- process_source: bfloat16 [512, 512], replicated, may hold values from -0.25 to 0.25
- process_dest: bfloat16 [512, 512], replicated, may hold values from -0.25 to 0.25
- process_output: bfloat16 [512, 512], replicated, may hold values from -0.25 to 0.25
- process_gain: float32 [512], replicated, may hold values from 0.5 to 1.5
Outputs:
- grid_grad: bfloat16 [16384, 512], P(('patch', 'group'))
- mesh_grad: bfloat16 [8192, 512], P(('patch', 'group'))
Inputs may be any that keep to these rules, and one draw needn't show every extreme that they name: `halo_rows`: a block's entries are rows of its own grid nodes. `encoder_sender`: rows of the block's extended grid table. `encoder_target`: rows of the block's own mesh nodes. The first encoder_count slots of a block are edges, the rest padding; some block is full in every draw. `process_sender`: rows of the block's sender table: its own mesh nodes, then the coarse nodes of its group. `process_target`: rows of the block's own mesh nodes. The first process_count slots of a block are edges, the rest padding; some block is full in every draw.
All inputs are finite; a program needn't handle non-finite values.
Results may differ from a plain program's by a relative error of at most 0.01.
Values may be sent and summed in bfloat16 or wider, within the bound.
No kernel may reach another device: no remote copies, remote signals or barrier semaphores. Data moves between devices by JAX's collectives and lax.ppermute only.
A program may use at most 64 MiB of HBM per device.

v0:
```python
import jax
import jax.numpy as jnp
from jax import lax
from jax.sharding import PartitionSpec as P

EPSILON = 1e-05


def padded_2(x, sides, width):
    for axis, dim in sides:
        size, length = (lax.axis_size(axis), x.shape[dim])
        up = [(i, (i + 1) % size) for i in range(size)]
        down = [(j, i) for i, j in up]
        last = lax.slice_in_dim(x, length - width, length, axis=dim)
        initial = lax.slice_in_dim(x, 0, width, axis=dim)
        before = lax.ppermute(last, axis, up)
        after = lax.ppermute(initial, axis, down)
        x = jnp.concatenate([before, x, after], axis=dim)
    return x


def silu_slope(values):
    logistic = jax.nn.sigmoid(values)
    return logistic * (1.0 + values * (1.0 - logistic))


def norm_forward(values, norm_gain):
    center = values - jnp.mean(values, axis=-1, keepdims=True)
    inverse = lax.rsqrt(jnp.mean(center * center, axis=-1, keepdims=True) + EPSILON)
    normed = center * inverse
    return (normed * norm_gain, normed, inverse)


def norm_backward(grad_out, normed, inverse, norm_gain):
    scaled = grad_out * norm_gain
    return inverse * (
        scaled
        - jnp.mean(scaled, axis=-1, keepdims=True)
        - normed * jnp.mean(scaled * normed, axis=-1, keepdims=True)
    )


def edge_forward(source, dest_proj, sender, target, live_count, out_weight, mesh_count):
    preact = source[sender] + dest_proj[target]
    hidden = jax.nn.silu(preact).astype(jnp.bfloat16)
    message = jnp.dot(hidden, out_weight, preferred_element_type=jnp.float32).astype(jnp.bfloat16)
    live_slots = jnp.arange(sender.shape[0], dtype=jnp.int32) < live_count
    onehot = (
        (target[None, :] == jnp.arange(mesh_count, dtype=jnp.int32)[:, None]) & live_slots[None, :]
    ).astype(jnp.bfloat16)
    gathered = jnp.dot(onehot, message, preferred_element_type=jnp.float32)
    return (gathered, preact, onehot, live_slots)


def edge_backward(
    grad_gathered, preact, onehot, live_slots, sender, target, out_weight, table_rows
):
    grad_message = jnp.where(live_slots[:, None], grad_gathered[target], 0.0).astype(jnp.bfloat16)
    grad_hidden = jnp.dot(grad_message, out_weight.T, preferred_element_type=jnp.float32)
    grad_preact = (grad_hidden * silu_slope(preact)).astype(jnp.bfloat16)
    chooser = (sender[None, :] == jnp.arange(table_rows, dtype=jnp.int32)[:, None]).astype(
        jnp.bfloat16
    )
    grad_source = jnp.dot(chooser, grad_preact, preferred_element_type=jnp.float32)
    grad_dest = jnp.dot(onehot, grad_preact, preferred_element_type=jnp.float32)
    return (grad_source, grad_dest)


def encoder_pass(
    extended,
    mesh_rows,
    sender,
    target,
    live_count,
    source_weight,
    dest_weight,
    out_weight,
    norm_gain,
):
    source = jnp.dot(extended, source_weight, preferred_element_type=jnp.float32)
    dest_proj = jnp.dot(mesh_rows, dest_weight, preferred_element_type=jnp.float32)
    gathered, preact, onehot, live_slots = edge_forward(
        source, dest_proj, sender, target, live_count, out_weight, mesh_rows.shape[0]
    )
    shifted, normed, inverse = norm_forward(gathered, norm_gain)
    updated = (mesh_rows.astype(jnp.float32) + shifted).astype(jnp.bfloat16)
    return (updated, (preact, onehot, live_slots, normed, inverse))


def encoder_backward(
    grad_updated, stored, table_rows, sender, target, dest_weight, out_weight, norm_gain
):
    preact, onehot, live_slots, normed, inverse = stored
    grad_gathered = norm_backward(grad_updated, normed, inverse, norm_gain)
    grad_source, grad_dest = edge_backward(
        grad_gathered, preact, onehot, live_slots, sender, target, out_weight, table_rows
    )
    mesh_grad = grad_updated + jnp.dot(
        grad_dest.astype(jnp.bfloat16), dest_weight.T, preferred_element_type=jnp.float32
    )
    return (mesh_grad, grad_source.astype(jnp.bfloat16))


def process_grads(
    updated,
    coarse_proj,
    sender,
    target,
    live_count,
    cotangent,
    source_weight,
    dest_weight,
    out_weight,
    norm_gain,
):
    local_proj = jnp.dot(updated, source_weight, preferred_element_type=jnp.float32)
    source = jnp.concatenate([local_proj, coarse_proj], axis=0)
    dest_proj = jnp.dot(updated, dest_weight, preferred_element_type=jnp.float32)
    gathered, preact, onehot, live_slots = edge_forward(
        source, dest_proj, sender, target, live_count, out_weight, updated.shape[0]
    )
    unused, normed, inverse = norm_forward(gathered, norm_gain)
    grad_out = cotangent.astype(jnp.float32)
    grad_gathered = norm_backward(grad_out, normed, inverse, norm_gain)
    grad_source, grad_dest = edge_backward(
        grad_gathered, preact, onehot, live_slots, sender, target, out_weight, source.shape[0]
    )
    mesh_count = updated.shape[0]
    grad_local = grad_out + jnp.dot(
        grad_source[:mesh_count].astype(jnp.bfloat16),
        source_weight.T,
        preferred_element_type=jnp.float32,
    )
    grad_local = grad_local + jnp.dot(
        grad_dest.astype(jnp.bfloat16), dest_weight.T, preferred_element_type=jnp.float32
    )
    return (grad_local, grad_source[mesh_count:])


def on_device(
    grid_latent,
    mesh_latent,
    cotangent,
    halo_rows,
    encoder_sender,
    encoder_target,
    encoder_count,
    process_sender,
    process_target,
    process_count,
    encoder_source,
    encoder_dest,
    encoder_output,
    encoder_gain,
    process_source,
    process_dest,
    process_output,
    process_gain,
):
    rim_size = halo_rows.shape[0] // 2
    grid_rows = grid_latent.shape[0]
    outgoing = grid_latent[halo_rows]
    padded = padded_2(outgoing, (("patch", 0),), rim_size)
    extended = jnp.concatenate([grid_latent, padded[:rim_size], padded[3 * rim_size :]], axis=0)
    updated, stored = encoder_pass(
        extended,
        mesh_latent,
        encoder_sender,
        encoder_target,
        encoder_count[0],
        encoder_source,
        encoder_dest,
        encoder_output,
        encoder_gain,
    )
    coarse_rows = mesh_latent.shape[0] // 16
    coarse_proj = jnp.dot(
        lax.all_gather(updated[:coarse_rows], "group", axis=0, tiled=True),
        process_source,
        preferred_element_type=jnp.float32,
    )
    grad_local, grad_coarse = process_grads(
        updated,
        coarse_proj,
        process_sender,
        process_target,
        process_count[0],
        cotangent,
        process_source,
        process_dest,
        process_output,
        process_gain,
    )
    back_weight = process_source.astype(jnp.float32).T
    coarse_grad = lax.psum_scatter(
        jnp.dot(
            grad_coarse,
            back_weight,
            precision=lax.Precision.HIGHEST,
            preferred_element_type=jnp.float32,
        ),
        "group",
        scatter_dimension=0,
        tiled=True,
    )
    grad_updated = grad_local.at[:coarse_rows].add(coarse_grad)
    mesh_grad, source_grads = encoder_backward(
        grad_updated,
        stored,
        extended.shape[0],
        encoder_sender,
        encoder_target,
        encoder_dest,
        encoder_output,
        encoder_gain,
    )
    own_grad = jnp.dot(
        source_grads[:grid_rows], encoder_source.T, preferred_element_type=jnp.float32
    )
    returned = padded_2(source_grads[grid_rows:], (("patch", 0),), rim_size)
    peer_sources = jnp.concatenate([returned[:rim_size], returned[3 * rim_size :]], axis=0)
    from_peers = jnp.dot(peer_sources, encoder_source.T, preferred_element_type=jnp.float32)
    grid_grad = own_grad.at[halo_rows].add(from_peers)
    return (grid_grad.astype(jnp.bfloat16), mesh_grad.astype(jnp.bfloat16))


def solution(mesh):
    return jax.shard_map(
        on_device,
        mesh=mesh,
        in_specs=(
            P(("patch", "group"), None),
            P(("patch", "group"), None),
            P(("patch", "group"), None),
            P(("patch", "group")),
            P(("patch", "group")),
            P(("patch", "group")),
            P(("patch", "group")),
            P(("patch", "group")),
            P(("patch", "group")),
            P(("patch", "group")),
            P(),
            P(),
            P(),
            P(),
            P(),
            P(),
            P(),
            P(),
        ),
        out_specs=(P(("patch", "group"), None), P(("patch", "group"), None)),
        check_vma=False,
    )
```

profile of v0, /device:TPU:1, one launch (start us, length us, event | category | flops | bytes accessed | tf_op | source)
XLA Modules:
  0.0 108.4 jit_solution(11747875148235382991)
XLA Ops:
  7.2 0.0 copy-start
  7.2 0.0 copy-start.20
  7.2 0.0 copy-start.16
  7.2 0.0 copy-start.18
  7.2 0.0 copy-start.10
  7.2 0.0 copy-start.7
  7.2 0.0 reduce-scatter.2.cloned.1.call-start
  7.3 0.8 compare_select_fusion.4
  8.1 0.6 copy-done.13
  8.7 2.3 %gather_fusion = bf16[256,512]{1,0:T(8,128)(2,1)S(1)} fusion(bf16[512,512]{1,0:T(8,128)(2,1)} %param.20, s32[1024]{0:T(1024)S(1)} %pad_clamp_fusion.4), kind=kCustom, calls=%fused_computation | custom fusion | bytes 525312 | tf_op jit(solution)/shard_map/gather | solution.py:162
  11.0 2.6 %collective-permute-start = (bf16[128,512]{1,0:T(8,128)(2,1)S(1)}, bf16[128,512]{1,0:T(8,128)(2,1)S(1)}, u32[]{:S(2)}, u32[]{:S(2)}) collective-permute-start(bf16[128,512]{1,0:T(8,128)(2,1)S(1)} %get-tuple-element.20), channel_id=1, source_target_pairs={{0,4},{4,8},{8,12},{12,16},{16,20},{20,24},{24,28},{28,0},{1,5},{5... | collective-permute-start | bytes 393224 | tf_op jit(solution)/shard_map/ppermute | solution.py:16
  13.7 0.0 collective-permute-start.1
  15.0 0.0 copy-done.20
  15.0 0.0 copy-start.24
  15.1 0.3 fusion.69
  15.4 0.0 copy-start.22
  15.5 0.0 copy-start.2
  15.5 3.1 %gather_fusion.2 = f32[768,512]{1,0:T(8,128)} fusion(f32[256,512]{1,0:T(8,128)S(1)} %fusion.69, s32[1024]{0:T(1024)S(1)} %pad_clamp_fusion.2), kind=kCustom, calls=%fused_computation.2 | custom fusion | bytes 3148800 | tf_op jit(solution)/shard_map/gather | solution.py:44
  18.6 0.0 collective-permute-done
  18.6 0.0 collective-permute-done.1
  18.6 0.6 fusion.7
  19.2 3.1 %gather_fusion.1 = f32[768,512]{1,0:T(8,128)} fusion(f32[768,512]{1,0:T(8,128)S(1)} %fusion.7, s32[1024]{0:T(1024)S(1)} %pad_clamp_fusion.3), kind=kCustom, calls=%fused_computation.1 | custom fusion | bytes 3148800 | tf_op jit(solution)/shard_map/gather | solution.py:44
  22.3 2.9 %fusion.67 = (f32[256]{0:T(256)S(1)}, f32[256,512]{1,0:T(8,128)S(1)}) fusion(bf16[512,512]{1,0:T(8,128)(2,1)} %param.32, f32[768,512]{1,0:T(8,128)} %gather_fusion.1, f32[768,512]{1,0:T(8,128)} %gather_fusion.2, s32[768]{0:T(1024)S(1)} %copy-done.18, pred[768]{0:T(1024)(128)(4,1)S(1)} %iota_compare_fusion.9), kind=kOutput, calls=%fused_computation.111 | convolution fusion | flops 607256320 | bytes 4199168 | tf_op jit(solution)/shard_map/dot_general | solution.py:51
  25.2 0.0 copy-start.1
  25.2 0.2 multiply_reduce_fusion.2
  25.5 0.0 copy-start.4
  25.5 0.2 add_convert_fusion
  25.7 10.7 %all_gather.3 = bf16[64,512]{1,0:T(8,128)(2,1)S(1)} all-gather(bf16[16,512]{1,0:T(8,128)(2,1)S(1)} %slice.72), channel_id=1, replica_groups=mesh['patch'=8,'group'=4] {'group'}, dimensions={0}, use_global_device_ids=true | all-gather | bytes 81920 | tf_op jit(solution)/shard_map/all_gather | solution.py:178
  36.4 0.3 fusion.70
  36.7 0.2 fusion.71
  36.9 0.3 fusion.72
  37.3 3.1 %gather_fusion.3 = f32[768,512]{1,0:T(8,128)} fusion(f32[320,512]{1,0:T(8,128)S(1)} %pad_maximum_fusion, s32[1024]{0:T(1024)S(1)} %pad_clamp_fusion.1), kind=kCustom, calls=%fused_computation.3 | custom fusion | bytes 3148800 | tf_op jit(solution)/shard_map/gather | solution.py:44
  40.4 3.1 %gather_fusion.4 = f32[768,512]{1,0:T(8,128)} fusion(f32[256,512]{1,0:T(8,128)S(1)} %fusion.72, s32[1024]{0:T(1024)S(1)} %pad_clamp_fusion), kind=kCustom, calls=%fused_computation.4 | custom fusion | bytes 3148800 | tf_op jit(solution)/shard_map/gather | solution.py:44
  43.5 2.9 %fusion.68 = (f32[256]{0:T(256)S(1)}, f32[256,512]{1,0:T(8,128)S(1)}) fusion(bf16[512,512]{1,0:T(8,128)(2,1)} %param.36, f32[768,512]{1,0:T(8,128)} %gather_fusion.3, f32[768,512]{1,0:T(8,128)} %gather_fusion.4, s32[768]{0:T(1024)S(1)} %copy-done.10, pred[768]{0:T(1024)(128)(4,1)S(1)} %iota_compare_fusion.8), kind=kOutput, calls=%fused_computation.112 | convolution fusion | flops 607256320 | bytes 4199168 | tf_op jit(solution)/shard_map/dot_general | solution.py:51
  46.4 0.2 multiply_reduce_fusion.1
  46.7 0.2 fusion.31
  46.9 0.2 fusion.33
  47.1 3.3 %gather_fusion.5 = bf16[768,512]{1,0:T(8,128)(2,1)} fusion(bf16[256,512]{1,0:T(8,128)(2,1)S(1)} %fusion.33, s32[1024]{0:T(1024)S(1)} %pad_clamp_fusion), kind=kCustom, calls=%fused_computation.5 | custom fusion | bytes 1575936 | tf_op jit(solution)/shard_map/gather | solution.py:58
  50.5 3.2 %multiply_convert_fusion.1 = bf16[768,512]{1,0:T(8,128)(2,1)S(1)} fusion(bf16[512,512]{1,0:T(8,128)(2,1)} %param.36, bf16[768,512]{1,0:T(8,128)(2,1)} %gather_fusion.5, pred[768]{0:T(1024)(128)(4,1)S(1)} %iota_compare_fusion.8, f32[768,512]{1,0:T(8,128)} %gather_fusion.3, f32[768,512]{1,0:T(8,128)} %gather_fusion.4), kind=kOutput, calls=%fused_computation.12 | convolution fusion | flops 406978560 | bytes 5243648 | tf_op jit(solution)/shard_map/dot_general | solution.py:59
  53.7 0.9 copy-done.6
  54.6 0.4 fusion.6
  55.0 1.3 %fusion.54 = f32[64,512]{1,0:T(8,128)} fusion(bf16[512,512]{1,0:T(8,128)(2,1)S(1)} %copy-done.1, f32[320,512]{1,0:T(8,128)S(1)} %fusion.6), kind=kOutput, calls=%fused_computation.79 | convolution fusion | flops 201326592 | bytes 786432 | tf_op jit(solution)/shard_map/dot_general | solution.py:196
  56.3 0.3 convolution_add_fusion.2
  56.6 0.0 reduce-scatter.2.cloned.1.call-update
  56.6 1.7 %convolution_add_fusion.1 = f32[256,512]{1,0:T(8,128)S(1)} fusion(f32[256,512]{1,0:T(8,128)S(1)} %convolution_add_fusion.2, bf16[512,512]{1,0:T(8,128)(2,1)S(1)} %copy-done.4, bf16[768,512]{1,0:T(8,128)(2,1)} %copy-done.6, s32[768]{0:T(1024)S(1)} %copy-done.10, pred[768]{0:T(1024)(128)(4,1)} %copy-done.22), kind=kOutput, calls=%fused_computation.24 | convolution fusion | flops 336199680 | bytes 2363136 | tf_op jit(solution)/shard_map/dot_general | solution.py:134
  58.4 19.3 %reduce-scatter.2.cloned.1.call-done = f32[16,512]{1,0:T(8,128)} async-done(((f32[64,512]{1,0:T(8,128)}), f32[16,512]{1,0:T(8,128)}) %reduce-scatter.2.cloned.1.call-update) | async-done | bytes 32784 | tf_op jit(solution)/shard_map/reduce_scatter | solution.py:195
  77.7 0.8 fusion.56
  78.5 0.2 multiply_reduce_fusion.3
  78.7 0.2 subtract_multiply_fusion
  78.9 0.0 copy-start.23
  79.0 2.7 %gather_fusion.6 = bf16[768,512]{1,0:T(8,128)(2,1)S(1)} fusion(bf16[256,512]{1,0:T(8,128)(2,1)S(1)} %subtract_multiply_fusion, s32[1024]{0:T(1024)S(1)} %pad_clamp_fusion.2), kind=kCustom, calls=%fused_computation.6 | custom fusion | bytes 1575936 | tf_op jit(solution)/shard_map/gather | solution.py:58
  81.7 0.0 copy-start.8
  81.7 0.0 copy-start.19
  81.7 3.7 %multiply_convert_fusion = bf16[768,512]{1,0:T(8,128)(2,1)} fusion(bf16[512,512]{1,0:T(8,128)(2,1)S(1)} %copy-done.23, bf16[768,512]{1,0:T(8,128)(2,1)S(1)} %gather_fusion.6, pred[768]{0:T(1024)(128)(4,1)S(1)} %copy-done.25, f32[768,512]{1,0:T(8,128)} %gather_fusion.1, f32[768,512]{1,0:T(8,128)} %gather_fusion.2), kind=kOutput, calls=%fused_computation.10 | convolution fusion | flops 406978560 | bytes 5243648 | tf_op jit(solution)/shard_map/dot_general | solution.py:59
  85.5 2.5 %fusion.4 = bf16[256,512]{1,0:T(8,128)(2,1)} fusion(f32[256,512]{1,0:T(8,128)S(1)} %fusion.56, bf16[512,512]{1,0:T(8,128)(2,1)S(1)} %copy-done.8, bf16[768,512]{1,0:T(8,128)(2,1)} %multiply_convert_fusion, s32[768]{0:T(1024)S(1)} %copy-done.19, pred[768]{0:T(1024)(128)(4,1)S(1)} %copy-done.25), kind=kOutput, calls=%fused_computation.26 | convolution fusion | flops 336330752 | bytes 2100992 | tf_op jit(solution)/shard_map/dot_general | solution.py:98
  88.0 0.8 fusion.1
  88.8 4.1 %collective-permute-start.2 = (bf16[128,512]{1,0:T(8,128)(2,1)S(1)}, bf16[128,512]{1,0:T(8,128)(2,1)S(1)}, u32[]{:S(2)}, u32[]{:S(2)}) collective-permute-start(bf16[128,512]{1,0:T(8,128)(2,1)S(1)} %get-tuple-element.18), channel_id=1, source_target_pairs={{0,4},{4,8},{8,12},{12,16},{16,20},{20,24},{24,28},{28,0},{1,5},{5... | collective-permute-start | bytes 393224 | tf_op jit(solution)/shard_map/ppermute | solution.py:16
  92.9 0.0 collective-permute-start.3
  92.9 0.5 fusion.35
  93.4 1.5 %collective-permute-done.2 = bf16[128,512]{1,0:T(8,128)(2,1)S(1)} collective-permute-done((bf16[128,512]{1,0:T(8,128)(2,1)S(1)}, bf16[128,512]{1,0:T(8,128)(2,1)S(1)}, u32[]{:S(2)}, u32[]{:S(2)}) %collective-permute-start.2) | collective-permute-done | bytes 131104 | tf_op jit(solution)/shard_map/ppermute | solution.py:16
  94.9 3.0 %collective-permute-done.3 = bf16[128,512]{1,0:T(8,128)(2,1)S(1)} collective-permute-done((bf16[128,512]{1,0:T(8,128)(2,1)S(1)}, bf16[128,512]{1,0:T(8,128)(2,1)S(1)}, u32[]{:S(2)}, u32[]{:S(2)}) %collective-permute-start.3) | collective-permute-done | bytes 131104 | tf_op jit(solution)/shard_map/ppermute | solution.py:17
  97.9 0.3 fusion.50
  98.2 2.5 %scatter_fusion = f32[512,512]{1,0:T(8,128)S(1)} fusion(f32[512,512]{1,0:T(8,128)S(1)} %fusion.35, s32[256]{0:T(256)S(1)} %copy-done.14, f32[256,512]{1,0:T(8,128)S(1)} %fusion.50), kind=kCustom, calls=%fused_computation.7 | custom fusion | flops 131072 | bytes 1573888 | tf_op jit(solution)/shard_map/scatter-add | solution.py:223
  100.7 0.9 convert_element_type.67
  (59 shorter events, 0.3 us)
Async XLA Ops:
  7.2 11.5 %copy-start = (bf16[512,512]{1,0:T(8,128)(2,1)S(1)}, bf16[512,512]{1,0:T(8,128)(2,1)}, u32[]{:S(2)}) copy-start(bf16[512,512]{1,0:T(8,128)(2,1)} %param.30) | copy-start | bytes 1572868
  7.2 7.8 %copy-start.20 = (s32[768]{0:T(1024)S(1)}, s32[768]{0:T(1024)}, u32[]{:S(2)}) copy-start(s32[768]{0:T(1024)} %param.24) | copy-start | bytes 9220
  7.2 7.8 %copy-start.16 = (s32[768]{0:T(1024)S(1)}, s32[768]{0:T(1024)}, u32[]{:S(2)}) copy-start(s32[768]{0:T(1024)} %param.27) | copy-start | bytes 9220
  7.2 7.9 %copy-start.18 = (s32[768]{0:T(1024)S(1)}, s32[768]{0:T(1024)}, u32[]{:S(2)}) copy-start(s32[768]{0:T(1024)} %param.25) | copy-start | bytes 9220
  7.2 7.9 %copy-start.10 = (s32[768]{0:T(1024)S(1)}, s32[768]{0:T(1024)}, u32[]{:S(2)}) copy-start(s32[768]{0:T(1024)} %param.28) | copy-start | bytes 9220
  7.2 7.9 %copy-start.7 = (bf16[512,512]{1,0:T(8,128)(2,1)S(1)}, bf16[512,512]{1,0:T(8,128)(2,1)}, u32[]{:S(2)}) copy-start(bf16[512,512]{1,0:T(8,128)(2,1)} %param.31) | copy-start | bytes 1572868
  7.2 7.9 %copy-start.5 = (bf16[256,512]{1,0:T(8,128)(2,1)S(1)}, bf16[256,512]{1,0:T(8,128)(2,1)}, u32[]{:S(2)}) copy-start(bf16[256,512]{1,0:T(8,128)(2,1)} %param.21) | copy-start | bytes 786436
  7.2 70.4 %reduce-scatter.2.cloned.1.call-start = ((), (), s32[]{:S(2)}) async-start(), calls=%async_computation.1 | async-start | bytes 163840 | tf_op jit(solution)/shard_map/reduce_scatter | solution.py:195
  8.1 0.6 copy-start.13
  11.0 7.6 %collective-permute-start = (bf16[128,512]{1,0:T(8,128)(2,1)S(1)}, bf16[128,512]{1,0:T(8,128)(2,1)S(1)}, u32[]{:S(2)}, u32[]{:S(2)}) collective-permute-start(bf16[128,512]{1,0:T(8,128)(2,1)S(1)} %get-tuple-element.20), channel_id=1, source_target_pairs={{0,4},{4,8},{8,12},{12,16},{16,20},{20,24},{24,28},{28,0},{1,5},{5... | collective-permute-start | bytes 393224 | tf_op jit(solution)/shard_map/ppermute | solution.py:16
  13.7 5.0 %collective-permute-start.1 = (bf16[128,512]{1,0:T(8,128)(2,1)S(1)}, bf16[128,512]{1,0:T(8,128)(2,1)S(1)}, u32[]{:S(2)}, u32[]{:S(2)}) collective-permute-start(bf16[128,512]{1,0:T(8,128)(2,1)S(1)} %get-tuple-element.21), channel_id=1, source_target_pairs={{4,0},{8,4},{12,8},{16,12},{20,16},{24,20},{28,24},{0,28},{5,1},{9... | collective-permute-start | bytes 393224 | tf_op jit(solution)/shard_map/ppermute | solution.py:17
  15.0 7.3 %copy-start.24 = (pred[768]{0:T(1024)(128)(4,1)}, pred[768]{0:T(1024)(128)(4,1)S(1)}, u32[]{:S(2)}) copy-start(pred[768]{0:T(1024)(128)(4,1)S(1)} %iota_compare_fusion.9) | copy-start | bytes 2308
  15.4 35.0 %copy-start.22 = (pred[768]{0:T(1024)(128)(4,1)}, pred[768]{0:T(1024)(128)(4,1)S(1)}, u32[]{:S(2)}) copy-start(pred[768]{0:T(1024)(128)(4,1)S(1)} %iota_compare_fusion.8) | copy-start | bytes 2308
  15.5 3.2 %copy-start.2 = (bf16[512,512]{1,0:T(8,128)(2,1)S(1)}, bf16[512,512]{1,0:T(8,128)(2,1)}, u32[]{:S(2)}) copy-start(bf16[512,512]{1,0:T(8,128)(2,1)} %param.20) | copy-start | bytes 1572868
  22.3 3.1 %copy-start.9 = (f32[512]{0:T(512)S(1)}, f32[512]{0:T(512)}, u32[]{:S(2)}) copy-start(f32[512]{0:T(512)} %param.33) | copy-start | bytes 6148
  25.2 11.2 %copy-start.1 = (bf16[512,512]{1,0:T(8,128)(2,1)S(1)}, bf16[512,512]{1,0:T(8,128)(2,1)}, u32[]{:S(2)}) copy-start(bf16[512,512]{1,0:T(8,128)(2,1)} %param.34) | copy-start | bytes 1572868
  25.4 11.5 %copy-start.11 = (f32[256]{0:T(256)}, f32[256]{0:T(256)S(1)}, u32[]{:S(2)}) copy-start(f32[256]{0:T(256)S(1)} %add_rsqrt_fusion.1) | copy-start | bytes 3076
  25.5 11.5 %copy-start.4 = (bf16[512,512]{1,0:T(8,128)(2,1)S(1)}, bf16[512,512]{1,0:T(8,128)(2,1)}, u32[]{:S(2)}) copy-start(bf16[512,512]{1,0:T(8,128)(2,1)} %param.35) | copy-start | bytes 1572868
  43.5 3.2 %copy-start.3 = (bf16[256,512]{1,0:T(8,128)(2,1)S(1)}, bf16[256,512]{1,0:T(8,128)(2,1)}, u32[]{:S(2)}) copy-start(bf16[256,512]{1,0:T(8,128)(2,1)} %param.22) | copy-start | bytes 786436
  43.5 3.2 %copy-start.15 = (f32[512]{0:T(512)S(1)}, f32[512]{0:T(512)}, u32[]{:S(2)}) copy-start(f32[512]{0:T(512)} %param.37) | copy-start | bytes 6148
  50.5 4.1 %copy-start.17 = (s32[768]{0:T(1024)S(1)}, s32[768]{0:T(1024)}, u32[]{:S(2)}) copy-start(s32[768]{0:T(1024)} %param.27) | copy-start | bytes 9220
  53.7 0.9 copy-start.6
  56.6 21.9 %copy-start.12 = (f32[256]{0:T(256)S(1)}, f32[256]{0:T(256)}, u32[]{:S(2)}) copy-start(f32[256]{0:T(256)} %copy-done.11) | copy-start | bytes 3076
  78.9 2.7 %copy-start.23 = (bf16[512,512]{1,0:T(8,128)(2,1)S(1)}, bf16[512,512]{1,0:T(8,128)(2,1)}, u32[]{:S(2)}) copy-start(bf16[512,512]{1,0:T(8,128)(2,1)} %param.32) | copy-start | bytes 1572868
  79.0 2.7 %copy-start.25 = (pred[768]{0:T(1024)(128)(4,1)S(1)}, pred[768]{0:T(1024)(128)(4,1)}, u32[]{:S(2)}) copy-start(pred[768]{0:T(1024)(128)(4,1)} %copy-done.24) | copy-start | bytes 2308
  81.7 3.8 %copy-start.8 = (bf16[512,512]{1,0:T(8,128)(2,1)S(1)}, bf16[512,512]{1,0:T(8,128)(2,1)}, u32[]{:S(2)}) copy-start(bf16[512,512]{1,0:T(8,128)(2,1)} %param.31) | copy-start | bytes 1572868
  81.7 3.8 %copy-start.19 = (s32[768]{0:T(1024)S(1)}, s32[768]{0:T(1024)}, u32[]{:S(2)}) copy-start(s32[768]{0:T(1024)} %param.25) | copy-start | bytes 9220
  85.5 2.5 %copy-start.21 = (s32[768]{0:T(1024)S(1)}, s32[768]{0:T(1024)}, u32[]{:S(2)}) copy-start(s32[768]{0:T(1024)} %param.24) | copy-start | bytes 9220
  85.5 2.5 %copy-start.26 = (bf16[768,512]{1,0:T(8,128)(2,1)S(1)}, bf16[768,512]{1,0:T(8,128)(2,1)}, u32[]{:S(2)}) copy-start(bf16[768,512]{1,0:T(8,128)(2,1)} %multiply_convert_fusion) | copy-start | bytes 2359300
  88.8 6.1 %collective-permute-start.2 = (bf16[128,512]{1,0:T(8,128)(2,1)S(1)}, bf16[128,512]{1,0:T(8,128)(2,1)S(1)}, u32[]{:S(2)}, u32[]{:S(2)}) collective-permute-start(bf16[128,512]{1,0:T(8,128)(2,1)S(1)} %get-tuple-element.18), channel_id=1, source_target_pairs={{0,4},{4,8},{8,12},{12,16},{16,20},{20,24},{24,28},{28,0},{1,5},{5... | collective-permute-start | bytes 393224 | tf_op jit(solution)/shard_map/ppermute | solution.py:16
  92.9 5.3 %copy-start.14 = (s32[256]{0:T(256)S(1)}, s32[256]{0:T(256)}, u32[]{:S(2)}) copy-start(s32[256]{0:T(256)} %copy-done.13) | copy-start | bytes 3076
  92.9 4.9 %collective-permute-start.3 = (bf16[128,512]{1,0:T(8,128)(2,1)S(1)}, bf16[128,512]{1,0:T(8,128)(2,1)S(1)}, u32[]{:S(2)}, u32[]{:S(2)}) collective-permute-start(bf16[128,512]{1,0:T(8,128)(2,1)S(1)} %get-tuple-element.19), channel_id=1, source_target_pairs={{4,0},{8,4},{12,8},{16,12},{20,16},{24,20},{28,24},{0,28},{5,1},{9... | collective-permute-start | bytes 393224 | tf_op jit(solution)/shard_map/ppermute | solution.py:17
Sparse Core Ops, SparseCore 0:
  56.8 20.8 reduce-scatter.1
where the time goes:
time: 109 us; the launch traced here: 108 us
  waiting for transfers between devices  23.8 us (22%)
  local copies, waits for them, and re-layouts  22.4 us (21%)
  matrix products  22.2 us (20%)
  between operations  15.9 us (15%)
  blocking collectives  10.7 us (10%)
  starting transfers between devices  6.83 us (6%)
  other arithmetic  6.52 us (6%)
    reduce_scatter x1, waiting for transfers between devices, on_device(): lax.psum_scatter(jnp.dot(grad_coarse, back_weight, precision=lax.Precisio...  19.3 us
    gather x4, local copies, waits for them, and re-layouts, edge_forward(): preact = source[sender] + dest_proj[target]  12.5 us
    all_gather x1, blocking collectives, on_device(): lax.all_gather(updated[:coarse_rows], 'group', axis=0, tiled=True)  10.7 us
    dot_general x2, matrix products, edge_backward(): jnp.dot(grad_message, out_weight.T, preferred_element_type=jnp.float32)  6.96 us
    ppermute x2, starting transfers between devices, padded_2(): before = lax.ppermute(last, axis, up)  6.78 us
    gather x2, local copies, waits for them, and re-layouts, edge_backward(): grad_gathered[target]  6 us
    dot_general x2, matrix products, edge_forward(): gathered = jnp.dot(onehot, message, preferred_element_type=jnp.float32)  5.79 us
    ppermute x2, waiting for transfers between devices, padded_2(): after = lax.ppermute(initial, axis, down)  3.03 us
  transfers between devices with their start and end apart: 5, of which 3 were waited for; matrix products, arithmetic and copies ran while one was open for 5% of the time, Pallas kernels for 0%

commit v1 on v0

--- a/solution.py
+++ b/solution.py
@@ -4,6 +4,18 @@
 from jax.sharding import PartitionSpec as P
 
 EPSILON = 1e-05
+
+
+def collect(shard, axis, dim):
+    ways, here, step = (lax.axis_size(axis), lax.axis_index(axis), shard.shape[dim])
+    line, have = (shard, 1)
+    while have < ways:
+        line = jnp.concatenate(
+            [line, lax.ppermute(line, axis, [(d, (d - have) % ways) for d in range(ways)])],
+            axis=dim,
+        )
+        have = 2 * have
+    return jnp.roll(line, here * step, axis=dim)
 
 
 def padded_2(x, sides, width):
@@ -175,7 +187,7 @@
     )
     coarse_rows = mesh_latent.shape[0] // 16
     coarse_proj = jnp.dot(
-        lax.all_gather(updated[:coarse_rows], "group", axis=0, tiled=True),
+        collect(updated[:coarse_rows], "group", 0),
         process_source,
         preferred_element_type=jnp.float32,
     )

time: 109 us -> 108 us (level)
  blocking collectives: 10.7 us -> 0 us
  local copies, waits for them, and re-layouts: 22.4 us -> 26.4 us
  starting transfers between devices: 6.83 us -> 10.2 us
  matrix products: 22.2 us -> 23.8 us
  other arithmetic: 6.52 us -> 7.66 us
    all_gather x1 -> x0, blocking collectives: 10.7 us -> none  [on_device(): lax.all_gather(updated[:coarse_rows], 'group', axis=0, tiled=True)]
    ppermute x0 -> x2, starting transfers between devices: none -> 3.39 us  [collect(): lax.ppermute(line, axis, [(d, (d - have) % ways) for d in range(ways)])]
    ppermute x0 -> x2, waiting for transfers between devices: none -> 3.04 us  [collect(): lax.ppermute(line, axis, [(d, (d - have) % ways) for d in range(ways)])]
    reduce_scatter x1, waiting for transfers between devices: 19.3 us -> 16.3 us  [on_device(): lax.psum_scatter(jnp.dot(grad_coarse, back_weight, precision=lax.Precisio...]
    unnamed x54 -> x66, local copies, waits for them, and re-layouts: 1.59 us -> 4.14 us
  transfers between devices with their start and end apart: 5 -> 7, of which waited for: 3 -> 4; matrix products, arithmetic and copies ran while one was open for 5% -> 10% of each run, Pallas kernels for 0% -> 0%
where the time goes in v1:
time: 108 us
  local copies, waits for them, and re-layouts  26.4 us (24%)
  matrix products  23.8 us (22%)
  waiting for transfers between devices  23.8 us (22%)
  between operations  15.9 us (15%)
  starting transfers between devices  10.2 us (9%)
  other arithmetic  7.66 us (7%)
    reduce_scatter x1, waiting for transfers between devices, on_device(): lax.psum_scatter(jnp.dot(grad_coarse, back_weight, precision=lax.Precisio...  16.3 us
    gather x4, local copies, waits for them, and re-layouts, edge_forward(): preact = source[sender] + dest_proj[target]  12.6 us
    dot_general x2, matrix products, edge_backward(): jnp.dot(grad_message, out_weight.T, preferred_element_type=jnp.float32)  6.8 us
    ppermute x2, starting transfers between devices, padded_2(): before = lax.ppermute(last, axis, up)  6.76 us
    gather x2, local copies, waits for them, and re-layouts, edge_backward(): grad_gathered[target]  6.02 us
    dot_general x2, matrix products, edge_forward(): gathered = jnp.dot(onehot, message, preferred_element_type=jnp.float32)  5.71 us
    unnamed x66, local copies, waits for them, and re-layouts  4.14 us
    ppermute x2, starting transfers between devices, collect(): lax.ppermute(line, axis, [(d, (d - have) % ways) for d in range(ways)])  3.39 us
  transfers between devices with their start and end apart: 7, of which 4 were waited for; matrix products, arithmetic and copies ran while one was open for 10% of the time, Pallas kernels for 0%

profile of v1, /device:TPU:1, one launch (start us, length us, event | category | flops | bytes accessed | tf_op | source)
XLA Modules:
  0.0 107.8 jit_solution(4593766827617686264)
XLA Ops:
  7.2 0.0 copy-start
  7.2 0.0 copy-start.21
  7.2 0.0 copy-start.17
  7.2 0.0 copy-start.7
  7.2 0.0 reduce-scatter.2.cloned.1.call-start
  7.3 0.8 compare_select_fusion.4
  8.1 2.3 %gather_fusion = bf16[256,512]{1,0:T(8,128)(2,1)S(1)} fusion(bf16[512,512]{1,0:T(8,128)(2,1)} %param.20, s32[1024]{0:T(1024)S(1)} %pad_clamp_fusion.4), kind=kCustom, calls=%fused_computation | custom fusion | bytes 525312 | tf_op jit(solution)/shard_map/gather | solution.py:174
  10.4 2.6 %collective-permute-start = (bf16[128,512]{1,0:T(8,128)(2,1)S(1)}, bf16[128,512]{1,0:T(8,128)(2,1)S(1)}, u32[]{:S(2)}, u32[]{:S(2)}) collective-permute-start(bf16[128,512]{1,0:T(8,128)(2,1)S(1)} %get-tuple-element.22), channel_id=1, source_target_pairs={{0,4},{4,8},{8,12},{12,16},{16,20},{20,24},{24,28},{28,0},{1,5},{5... | collective-permute-start | bytes 393224 | tf_op jit(solution)/shard_map/ppermute | solution.py:28
  14.5 0.3 fusion.73
  14.8 0.6 iota_compare_fusion.8
  15.4 3.1 %gather_fusion.2 = f32[768,512]{1,0:T(8,128)} fusion(f32[256,512]{1,0:T(8,128)S(1)} %fusion.73, s32[1024]{0:T(1024)S(1)} %get-tuple-element.30), kind=kCustom, calls=%fused_computation.2 | custom fusion | bytes 3148800 | tf_op jit(solution)/shard_map/gather | solution.py:56
  18.5 0.6 pad_clamp_fusion
  19.1 0.7 copy-done.27
  19.8 1.5 %fusion.7 = f32[768,512]{1,0:T(8,128)S(1)} fusion(bf16[512,512]{1,0:T(8,128)(2,1)S(1)} %copy-done, bf16[128,512]{1,0:T(8,128)(2,1)} %collective-permute-done.1, bf16[128,512]{1,0:T(8,128)(2,1)} %copy-done.27, bf16[512,512]{1,0:T(8,128)(2,1)S(1)} %copy-done.2), kind=kOutput, calls=%fused_computation.32 | convolution fusion | flops 405012480 | bytes 2883584 | tf_op jit(solution)/shard_map/dot_general | solution.py:92
  21.3 0.0 copy-start.25
  21.4 3.1 %gather_fusion.1 = f32[768,512]{1,0:T(8,128)} fusion(f32[768,512]{1,0:T(8,128)S(1)} %fusion.7, s32[1024]{0:T(1024)S(1)} %get-tuple-element.31), kind=kCustom, calls=%fused_computation.1 | custom fusion | bytes 3148800 | tf_op jit(solution)/shard_map/gather | solution.py:56
  24.5 2.8 %fusion.71 = (f32[256]{0:T(256)S(1)}, f32[256,512]{1,0:T(8,128)S(1)}) fusion(bf16[512,512]{1,0:T(8,128)(2,1)S(1)} %copy-done.25, f32[768,512]{1,0:T(8,128)} %gather_fusion.1, f32[768,512]{1,0:T(8,128)} %gather_fusion.2, s32[768]{0:T(1024)S(1)} %copy-done.19, pred[768]{0:T(1024)(128)(4,1)S(1)} %iota_compare_fusion.9), kind=kOutput, calls=%fused_computation.122 | convolution fusion | flops 607256320 | bytes 4199168 | tf_op jit(solution)/shard_map/dot_general | solution.py:63
  27.3 0.0 copy-start.1
  27.3 0.2 multiply_reduce_fusion.2
  27.5 0.2 add_convert_fusion
  27.7 0.6 fusion.69
  28.3 3.3 %collective-permute-start.2 = (bf16[16,512]{1,0:T(8,128)(2,1)S(1)}, bf16[16,512]{1,0:T(8,128)(2,1)S(1)}, u32[]{:S(2)}, u32[]{:S(2)}) collective-permute-start(bf16[16,512]{1,0:T(8,128)(2,1)S(1)} %get-tuple-element.20), channel_id=1, source_target_pairs={{0,3},{1,0},{2,1},{3,2},{4,7},{5,4},{6,5},{7,6},{8,11},{9,8},{10,9... | collective-permute-start | bytes 49160 | tf_op jit(solution)/shard_map/ppermute | solution.py:14
  31.7 0.3 fusion.75
  32.0 0.3 fusion.74
  32.3 3.1 %gather_fusion.4 = f32[768,512]{1,0:T(8,128)} fusion(f32[256,512]{1,0:T(8,128)S(1)} %fusion.75, s32[1024]{0:T(1024)S(1)} %get-tuple-element.28), kind=kCustom, calls=%fused_computation.4 | custom fusion | bytes 3148800 | tf_op jit(solution)/shard_map/gather | solution.py:56
  35.4 0.1 collective-permute-start.3
  35.5 0.6 constant_dynamic-update-slice_fusion.4
  36.1 3.0 %collective-permute-done.3 = bf16[32,512]{1,0:T(8,128)(2,1)S(1)} collective-permute-done((bf16[32,512]{1,0:T(8,128)(2,1)S(1)}, bf16[32,512]{1,0:T(8,128)(2,1)S(1)}, u32[]{:S(2)}, u32[]{:S(2)}) %collective-permute-start.3) | collective-permute-done | bytes 32800 | tf_op jit(solution)/shard_map/ppermute | solution.py:14
  39.1 0.6 constant_dynamic-update-slice_fusion.3
  39.8 0.6 constant_dynamic-update-slice_fusion.2
  40.4 0.6 constant_dynamic-update-slice_fusion.1
  41.0 0.6 constant_dynamic-update-slice_fusion
  41.6 1.0 fusion.56
  42.7 3.2 %gather_fusion.3 = f32[768,512]{1,0:T(8,128)} fusion(f32[320,512]{1,0:T(8,128)S(1)} %pad_maximum_fusion, s32[1024]{0:T(1024)} %get-tuple-element.29), kind=kCustom, calls=%fused_computation.3 | custom fusion | bytes 3148800 | tf_op jit(solution)/shard_map/gather | solution.py:56
  45.9 2.9 %fusion.72 = (f32[256]{0:T(256)S(1)}, f32[256,512]{1,0:T(8,128)S(1)}) fusion(bf16[512,512]{1,0:T(8,128)(2,1)} %param.36, f32[768,512]{1,0:T(8,128)} %gather_fusion.3, f32[768,512]{1,0:T(8,128)} %gather_fusion.4, s32[768]{0:T(1024)} %param.28, pred[768]{0:T(1024)(128)(4,1)} %iota_compare_fusion.8), kind=kOutput, calls=%fused_computation.123 | convolution fusion | flops 607256320 | bytes 4199168 | tf_op jit(solution)/shard_map/dot_general | solution.py:63
  48.9 0.2 multiply_reduce_fusion.1
  49.1 0.2 fusion.31
  49.4 0.2 fusion.33
  49.6 0.0 copy-start.24
  49.6 3.3 %gather_fusion.5 = bf16[768,512]{1,0:T(8,128)(2,1)} fusion(bf16[256,512]{1,0:T(8,128)(2,1)S(1)} %fusion.33, s32[1024]{0:T(1024)S(1)} %get-tuple-element.28), kind=kCustom, calls=%fused_computation.5 | custom fusion | bytes 1575936 | tf_op jit(solution)/shard_map/gather | solution.py:70
  53.0 3.0 %multiply_convert_fusion.1 = bf16[768,512]{1,0:T(8,128)(2,1)S(1)} fusion(bf16[512,512]{1,0:T(8,128)(2,1)S(1)} %copy-done.24, bf16[768,512]{1,0:T(8,128)(2,1)} %gather_fusion.5, pred[768]{0:T(1024)(128)(4,1)S(1)} %copy-done.23, f32[768,512]{1,0:T(8,128)} %gather_fusion.3, f32[768,512]{1,0:T(8,128)} %gather_fusion.4), kind=kOutput, calls=%fused_computation.12 | convolution fusion | flops 406978560 | bytes 5243648 | tf_op jit(solution)/shard_map/dot_general | solution.py:71
  56.0 0.9 copy-done.6
  56.9 0.4 fusion.6
  57.3 0.0 copy-start.11
  57.4 1.3 %fusion.54 = f32[64,512]{1,0:T(8,128)} fusion(bf16[512,512]{1,0:T(8,128)(2,1)S(1)} %copy-done.1, f32[320,512]{1,0:T(8,128)S(1)} %fusion.6), kind=kOutput, calls=%fused_computation.79 | convolution fusion | flops 201326592 | bytes 786432 | tf_op jit(solution)/shard_map/dot_general | solution.py:208
  58.6 0.3 convolution_add_fusion.2
  59.0 0.0 reduce-scatter.2.cloned.1.call-update
  59.0 1.7 %convolution_add_fusion.1 = f32[256,512]{1,0:T(8,128)S(1)} fusion(f32[256,512]{1,0:T(8,128)S(1)} %convolution_add_fusion.2, bf16[512,512]{1,0:T(8,128)(2,1)S(1)} %copy-done.4, bf16[768,512]{1,0:T(8,128)(2,1)} %copy-done.6, s32[768]{0:T(1024)S(1)} %copy-done.11, pred[768]{0:T(1024)(128)(4,1)} %iota_compare_fusion.8), kind=kOutput, calls=%fused_computation.24 | convolution fusion | flops 336199680 | bytes 2363136 | tf_op jit(solution)/shard_map/dot_general | solution.py:146
  60.7 16.3 %reduce-scatter.2.cloned.1.call-done = f32[16,512]{1,0:T(8,128)} async-done(((f32[64,512]{1,0:T(8,128)}), f32[16,512]{1,0:T(8,128)}) %reduce-scatter.2.cloned.1.call-update) | async-done | bytes 32784 | tf_op jit(solution)/shard_map/reduce_scatter | solution.py:207
  77.0 0.8 fusion.58
  77.8 0.2 multiply_reduce_fusion.3
  78.1 0.2 subtract_multiply_fusion
  78.3 0.0 copy-start.26
  78.3 2.7 %gather_fusion.6 = bf16[768,512]{1,0:T(8,128)(2,1)S(1)} fusion(bf16[256,512]{1,0:T(8,128)(2,1)S(1)} %subtract_multiply_fusion, s32[1024]{0:T(1024)S(1)} %get-tuple-element.30), kind=kCustom, calls=%fused_computation.6 | custom fusion | bytes 1575936 | tf_op jit(solution)/shard_map/gather | solution.py:70
  81.0 3.8 %multiply_convert_fusion = bf16[768,512]{1,0:T(8,128)(2,1)} fusion(bf16[512,512]{1,0:T(8,128)(2,1)S(1)} %copy-done.26, bf16[768,512]{1,0:T(8,128)(2,1)S(1)} %gather_fusion.6, pred[768]{0:T(1024)(128)(4,1)S(1)} %copy-done.29, f32[768,512]{1,0:T(8,128)} %gather_fusion.1, f32[768,512]{1,0:T(8,128)} %gather_fusion.2), kind=kOutput, calls=%fused_computation.10 | convolution fusion | flops 406978560 | bytes 5243648 | tf_op jit(solution)/shard_map/dot_general | solution.py:71
  84.8 2.5 %fusion.4 = bf16[256,512]{1,0:T(8,128)(2,1)} fusion(f32[256,512]{1,0:T(8,128)S(1)} %fusion.58, bf16[512,512]{1,0:T(8,128)(2,1)S(1)} %copy-done.8, bf16[768,512]{1,0:T(8,128)(2,1)} %multiply_convert_fusion, s32[768]{0:T(1024)S(1)} %copy-done.20, pred[768]{0:T(1024)(128)(4,1)S(1)} %copy-done.29), kind=kOutput, calls=%fused_computation.26 | convolution fusion | flops 336330752 | bytes 2100992 | tf_op jit(solution)/shard_map/dot_general | solution.py:110
  87.3 0.8 fusion.1
  88.1 4.1 %collective-permute-start.4 = (bf16[128,512]{1,0:T(8,128)(2,1)S(1)}, bf16[128,512]{1,0:T(8,128)(2,1)S(1)}, u32[]{:S(2)}, u32[]{:S(2)}) collective-permute-start(bf16[128,512]{1,0:T(8,128)(2,1)S(1)} %get-tuple-element.18), channel_id=1, source_target_pairs={{0,4},{4,8},{8,12},{12,16},{16,20},{20,24},{24,28},{28,0},{1,5},{5... | collective-permute-start | bytes 393224 | tf_op jit(solution)/shard_map/ppermute | solution.py:28
  92.3 0.5 fusion.35
  92.7 1.5 %collective-permute-done.4 = bf16[128,512]{1,0:T(8,128)(2,1)S(1)} collective-permute-done((bf16[128,512]{1,0:T(8,128)(2,1)S(1)}, bf16[128,512]{1,0:T(8,128)(2,1)S(1)}, u32[]{:S(2)}, u32[]{:S(2)}) %collective-permute-start.4) | collective-permute-done | bytes 131104 | tf_op jit(solution)/shard_map/ppermute | solution.py:28
  94.2 3.0 %collective-permute-done.5 = bf16[128,512]{1,0:T(8,128)(2,1)S(1)} collective-permute-done((bf16[128,512]{1,0:T(8,128)(2,1)S(1)}, bf16[128,512]{1,0:T(8,128)(2,1)S(1)}, u32[]{:S(2)}, u32[]{:S(2)}) %collective-permute-start.5) | collective-permute-done | bytes 131104 | tf_op jit(solution)/shard_map/ppermute | solution.py:29
  97.2 0.3 fusion.50
  97.6 2.5 %scatter_fusion = f32[512,512]{1,0:T(8,128)S(1)} fusion(f32[512,512]{1,0:T(8,128)S(1)} %fusion.35, s32[256]{0:T(256)S(1)} %copy-done.15, f32[256,512]{1,0:T(8,128)S(1)} %fusion.50), kind=kCustom, calls=%fused_computation.7 | custom fusion | flops 131072 | bytes 1573888 | tf_op jit(solution)/shard_map/scatter-add | solution.py:235
  100.1 0.9 convert_element_type.67
  (75 shorter events, 0.3 us)
Async XLA Ops:
  7.2 12.6 %copy-start = (bf16[512,512]{1,0:T(8,128)(2,1)S(1)}, bf16[512,512]{1,0:T(8,128)(2,1)}, u32[]{:S(2)}) copy-start(bf16[512,512]{1,0:T(8,128)(2,1)} %param.30) | copy-start | bytes 1572868
  7.2 7.2 %copy-start.21 = (s32[768]{0:T(1024)S(1)}, s32[768]{0:T(1024)}, u32[]{:S(2)}) copy-start(s32[768]{0:T(1024)} %param.24) | copy-start | bytes 9220
  7.2 7.2 %copy-start.17 = (s32[768]{0:T(1024)S(1)}, s32[768]{0:T(1024)}, u32[]{:S(2)}) copy-start(s32[768]{0:T(1024)} %param.27) | copy-start | bytes 9220
  7.2 7.3 %copy-start.19 = (s32[768]{0:T(1024)S(1)}, s32[768]{0:T(1024)}, u32[]{:S(2)}) copy-start(s32[768]{0:T(1024)} %param.25) | copy-start | bytes 9220
  7.2 7.3 %copy-start.10 = (s32[768]{0:T(1024)S(1)}, s32[768]{0:T(1024)}, u32[]{:S(2)}) copy-start(s32[768]{0:T(1024)} %param.28) | copy-start | bytes 9220
  7.2 7.3 %copy-start.7 = (bf16[512,512]{1,0:T(8,128)(2,1)S(1)}, bf16[512,512]{1,0:T(8,128)(2,1)}, u32[]{:S(2)}) copy-start(bf16[512,512]{1,0:T(8,128)(2,1)} %param.31) | copy-start | bytes 1572868
  7.2 7.3 %copy-start.5 = (bf16[256,512]{1,0:T(8,128)(2,1)S(1)}, bf16[256,512]{1,0:T(8,128)(2,1)}, u32[]{:S(2)}) copy-start(bf16[256,512]{1,0:T(8,128)(2,1)} %param.21) | copy-start | bytes 786436
  7.2 69.8 %reduce-scatter.2.cloned.1.call-start = ((), (), s32[]{:S(2)}) async-start(), calls=%async_computation.1 | async-start | bytes 163840 | tf_op jit(solution)/shard_map/reduce_scatter | solution.py:207
  8.1 6.4 %copy-start.14 = (s32[256]{0:T(256)}, s32[256]{0:T(256)S(1)}, u32[]{:S(2)}) copy-start(s32[256]{0:T(256)S(1)} %compare_select_fusion.4) | copy-start | bytes 3076
  10.4 8.7 %collective-permute-start = (bf16[128,512]{1,0:T(8,128)(2,1)S(1)}, bf16[128,512]{1,0:T(8,128)(2,1)S(1)}, u32[]{:S(2)}, u32[]{:S(2)}) collective-permute-start(bf16[128,512]{1,0:T(8,128)(2,1)S(1)} %get-tuple-element.22), channel_id=1, source_target_pairs={{0,4},{4,8},{8,12},{12,16},{16,20},{20,24},{24,28},{28,0},{1,5},{5... | collective-permute-start | bytes 393224 | tf_op jit(solution)/shard_map/ppermute | solution.py:28
  13.1 6.7 %collective-permute-start.1 = (bf16[128,512]{1,0:T(8,128)(2,1)S(1)}, bf16[128,512]{1,0:T(8,128)(2,1)}, u32[]{:S(2)}, u32[]{:S(2)}) collective-permute-start(bf16[128,512]{1,0:T(8,128)(2,1)S(1)} %get-tuple-element.23), channel_id=1, source_target_pairs={{4,0},{8,4},{12,8},{16,12},{20,16},{24,20},{28,24},{0,28},{5,1},{9... | collective-permute-start | bytes 393224 | tf_op jit(solution)/shard_map/ppermute | solution.py:29
  14.4 10.1 %copy-start.28 = (pred[768]{0:T(1024)(128)(4,1)}, pred[768]{0:T(1024)(128)(4,1)S(1)}, u32[]{:S(2)}) copy-start(pred[768]{0:T(1024)(128)(4,1)S(1)} %iota_compare_fusion.9) | copy-start | bytes 2308
  15.4 4.4 %copy-start.2 = (bf16[512,512]{1,0:T(8,128)(2,1)S(1)}, bf16[512,512]{1,0:T(8,128)(2,1)}, u32[]{:S(2)}) copy-start(bf16[512,512]{1,0:T(8,128)(2,1)} %param.20) | copy-start | bytes 1572868
  19.1 0.7 copy-start.27
  21.3 3.2 %copy-start.25 = (bf16[512,512]{1,0:T(8,128)(2,1)S(1)}, bf16[512,512]{1,0:T(8,128)(2,1)}, u32[]{:S(2)}) copy-start(bf16[512,512]{1,0:T(8,128)(2,1)} %param.32) | copy-start | bytes 1572868
  24.5 3.0 %copy-start.9 = (f32[512]{0:T(512)S(1)}, f32[512]{0:T(512)}, u32[]{:S(2)}) copy-start(f32[512]{0:T(512)} %param.33) | copy-start | bytes 6148
  27.3 4.4 %copy-start.4 = (bf16[512,512]{1,0:T(8,128)(2,1)S(1)}, bf16[512,512]{1,0:T(8,128)(2,1)}, u32[]{:S(2)}) copy-start(bf16[512,512]{1,0:T(8,128)(2,1)} %param.35) | copy-start | bytes 1572868
  27.3 4.7 %copy-start.1 = (bf16[512,512]{1,0:T(8,128)(2,1)S(1)}, bf16[512,512]{1,0:T(8,128)(2,1)}, u32[]{:S(2)}) copy-start(bf16[512,512]{1,0:T(8,128)(2,1)} %param.34) | copy-start | bytes 1572868
  27.5 0.8 copy-start.12
  28.3 7.1 %collective-permute-start.2 = (bf16[16,512]{1,0:T(8,128)(2,1)S(1)}, bf16[16,512]{1,0:T(8,128)(2,1)S(1)}, u32[]{:S(2)}, u32[]{:S(2)}) collective-permute-start(bf16[16,512]{1,0:T(8,128)(2,1)S(1)} %get-tuple-element.20), channel_id=1, source_target_pairs={{0,3},{1,0},{2,1},{3,2},{4,7},{5,4},{6,5},{7,6},{8,11},{9,8},{10,9... | collective-permute-start | bytes 49160 | tf_op jit(solution)/shard_map/ppermute | solution.py:14
  35.4 3.7 %collective-permute-start.3 = (bf16[32,512]{1,0:T(8,128)(2,1)S(1)}, bf16[32,512]{1,0:T(8,128)(2,1)S(1)}, u32[]{:S(2)}, u32[]{:S(2)}) collective-permute-start(bf16[32,512]{1,0:T(8,128)(2,1)S(1)} %pad_maximum_fusion.1), channel_id=1, source_target_pairs={{0,2},{1,3},{2,0},{3,1},{4,6},{5,7},{6,4},{7,5},{8,10},{9,11},{10,... | collective-permute-start | bytes 98312 | tf_op jit(solution)/shard_map/ppermute | solution.py:14
  45.9 3.2 %copy-start.3 = (bf16[256,512]{1,0:T(8,128)(2,1)S(1)}, bf16[256,512]{1,0:T(8,128)(2,1)}, u32[]{:S(2)}) copy-start(bf16[256,512]{1,0:T(8,128)(2,1)} %param.22) | copy-start | bytes 786436
  45.9 3.2 %copy-start.16 = (f32[512]{0:T(512)S(1)}, f32[512]{0:T(512)}, u32[]{:S(2)}) copy-start(f32[512]{0:T(512)} %param.37) | copy-start | bytes 6148
  49.6 3.4 %copy-start.23 = (pred[768]{0:T(1024)(128)(4,1)S(1)}, pred[768]{0:T(1024)(128)(4,1)}, u32[]{:S(2)}) copy-start(pred[768]{0:T(1024)(128)(4,1)} %iota_compare_fusion.8) | copy-start | bytes 2308
  49.6 3.4 %copy-start.24 = (bf16[512,512]{1,0:T(8,128)(2,1)S(1)}, bf16[512,512]{1,0:T(8,128)(2,1)}, u32[]{:S(2)}) copy-start(bf16[512,512]{1,0:T(8,128)(2,1)} %param.36) | copy-start | bytes 1572868
  53.0 4.0 %copy-start.18 = (s32[768]{0:T(1024)S(1)}, s32[768]{0:T(1024)}, u32[]{:S(2)}) copy-start(s32[768]{0:T(1024)} %param.27) | copy-start | bytes 9220
  56.0 0.9 copy-start.6
  57.3 1.6 %copy-start.11 = (s32[768]{0:T(1024)S(1)}, s32[768]{0:T(1024)}, u32[]{:S(2)}) copy-start(s32[768]{0:T(1024)} %param.28) | copy-start | bytes 9220
  59.0 18.8 %copy-start.13 = (f32[256]{0:T(256)S(1)}, f32[256]{0:T(256)}, u32[]{:S(2)}) copy-start(f32[256]{0:T(256)} %copy-done.12) | copy-start | bytes 3076
  78.3 2.7 %copy-start.26 = (bf16[512,512]{1,0:T(8,128)(2,1)S(1)}, bf16[512,512]{1,0:T(8,128)(2,1)}, u32[]{:S(2)}) copy-start(bf16[512,512]{1,0:T(8,128)(2,1)} %param.32) | copy-start | bytes 1572868
  78.3 2.7 %copy-start.29 = (pred[768]{0:T(1024)(128)(4,1)S(1)}, pred[768]{0:T(1024)(128)(4,1)}, u32[]{:S(2)}) copy-start(pred[768]{0:T(1024)(128)(4,1)} %copy-done.28) | copy-start | bytes 2308
  81.0 3.8 %copy-start.8 = (bf16[512,512]{1,0:T(8,128)(2,1)S(1)}, bf16[512,512]{1,0:T(8,128)(2,1)}, u32[]{:S(2)}) copy-start(bf16[512,512]{1,0:T(8,128)(2,1)} %param.31) | copy-start | bytes 1572868
  81.0 3.8 %copy-start.20 = (s32[768]{0:T(1024)S(1)}, s32[768]{0:T(1024)}, u32[]{:S(2)}) copy-start(s32[768]{0:T(1024)} %param.25) | copy-start | bytes 9220
  84.8 2.5 %copy-start.22 = (s32[768]{0:T(1024)S(1)}, s32[768]{0:T(1024)}, u32[]{:S(2)}) copy-start(s32[768]{0:T(1024)} %param.24) | copy-start | bytes 9220
  84.8 2.5 %copy-start.30 = (bf16[768,512]{1,0:T(8,128)(2,1)S(1)}, bf16[768,512]{1,0:T(8,128)(2,1)}, u32[]{:S(2)}) copy-start(bf16[768,512]{1,0:T(8,128)(2,1)} %multiply_convert_fusion) | copy-start | bytes 2359300
  88.1 6.1 %collective-permute-start.4 = (bf16[128,512]{1,0:T(8,128)(2,1)S(1)}, bf16[128,512]{1,0:T(8,128)(2,1)S(1)}, u32[]{:S(2)}, u32[]{:S(2)}) collective-permute-start(bf16[128,512]{1,0:T(8,128)(2,1)S(1)} %get-tuple-element.18), channel_id=1, source_target_pairs={{0,4},{4,8},{8,12},{12,16},{16,20},{20,24},{24,28},{28,0},{1,5},{5... | collective-permute-start | bytes 393224 | tf_op jit(solution)/shard_map/ppermute | solution.py:28
  92.3 5.3 %copy-start.15 = (s32[256]{0:T(256)S(1)}, s32[256]{0:T(256)}, u32[]{:S(2)}) copy-start(s32[256]{0:T(256)} %copy-done.14) | copy-start | bytes 3076
  92.3 5.0 %collective-permute-start.5 = (bf16[128,512]{1,0:T(8,128)(2,1)S(1)}, bf16[128,512]{1,0:T(8,128)(2,1)S(1)}, u32[]{:S(2)}, u32[]{:S(2)}) collective-permute-start(bf16[128,512]{1,0:T(8,128)(2,1)S(1)} %get-tuple-element.19), channel_id=1, source_target_pairs={{4,0},{8,4},{12,8},{16,12},{20,16},{24,20},{28,24},{0,28},{5,1},{9... | collective-permute-start | bytes 393224 | tf_op jit(solution)/shard_map/ppermute | solution.py:29
Sparse Core Ops, SparseCore 0:
  59.1 17.8 reduce-scatter.1
